TPU v7x, 256 devices: a whole 4x4x8 slice. The times are simulated.
256 devices in a mesh: dp: 16 (over z, core), expert: 16 (over y, x).
Axes of the slice: x: 4, y: 4, z: 8, core: 2. Of those that a mesh axis runs over, the one named last changes fastest.
Arguments:
- ssm_state: bfloat16 [1024, 16, 4096], P('expert', None, 'dp'), may hold values from -6 to 6
- conv_state: bfloat16 [1024, 3, 4096], P('expert', None, 'dp'), may hold values from -6 to 6
- new_slot: int32 [1024], replicated, may hold values from 0 to 1023, as said below
- conv_input: bfloat16 [1024, 4096], P('expert', 'dp'), may hold values from -6 to 6
- gate_input: bfloat16 [1024, 4096], P('expert', 'dp'), may hold values from -6 to 6
- conv_weight: float32 [4, 4096], P(None, 'dp'), may hold values from -3 to 3
- conv_bias: float32 [4096], P('dp'), may hold values from -3 to 3
- x_proj_weight: bfloat16 [4096, 288], P('dp'), may hold values from -0.09375 to 0.09375
- step_weight: bfloat16 [256, 4096], P(None, 'dp'), may hold values from -0.375 to 0.375
- step_bias: float32 [4096], P('dp'), may hold values from -3 to -0.5
- decay_log: float32 [16, 4096], P(None, 'dp'), may hold values from 0 to 2
- skip_gain: float32 [4096], P('dp'), may hold values from 0.5 to 1.5
- out_proj_weight: bfloat16 [4096, 4096], P('dp', 'expert'), may hold values from -0.09375 to 0.09375
- residual: bfloat16 [1024, 4096], P(None, 'expert'), may hold values from -6 to 6
- norm_gain: float32 [4096], replicated, may hold values from 0.1 to 1.9
- routes: int32 [1024, 2], replicated, may hold values from 0 to 15, all different within a row; in each aligned block of 64 rows (0 to 63, 64 to 127, ...) at most 20 rows name the same one
- gate_weight: float32 [1024, 2], replicated, may hold values from 0.1 to 0.9
- expert_gate: bfloat16 [16, 4096, 7168], P('expert', None, 'dp'), may hold values from -0.09375 to 0.09375
- expert_up: bfloat16 [16, 4096, 7168], P('expert', None, 'dp'), may hold values from -0.09375 to 0.09375
- expert_down: bfloat16 [16, 7168, 4096], P('expert', 'dp'), may hold values from -0.0625 to 0.0625
Outputs:
- ssm_new: bfloat16 [1024, 16, 4096], P('expert', None, 'dp')
- conv_new: bfloat16 [1024, 3, 4096], P('expert', None, 'dp')
- layer_out: bfloat16 [1024, 4096], P(None, 'expert')
Inputs may be any that keep to these rules, and one draw needn't show every extreme that they name: new_slot is a permutation of the 1024 slots; slot s belongs to expert index s // 64. Of the 64 old slots of one expert index, at most 8 get new slots of any one expert index, and exactly 8 those of some expert index; every expert index sends the same multiset of such counts. `routes`: each row names 2 different experts; within each aligned block of 64 rows (the rows of one expert index) no expert is named by more than 20 rows, a bound that some block reaches.
All inputs are finite; a program needn't handle non-finite values.
Results may differ from a plain program's by a relative error of at most 0.012.
Values may be sent and summed in bfloat16 or wider, within the bound.
A program may use at most 128 MiB of HBM per device.

v0:
```python
import jax
import jax.numpy as jnp
from jax import lax
from jax.sharding import PartitionSpec as P


def dp_total(values):
    return lax.psum(values, "dp")


def body(
    ssm_state,
    conv_state,
    new_slot,
    conv_input,
    gate_input,
    conv_weight,
    conv_bias,
    x_proj_weight,
    step_weight,
    step_bias,
    decay_log,
    skip_gain,
    out_proj_weight,
    residual,
    norm_gain,
    routes,
    gate_weight,
    expert_gate,
    expert_up,
    expert_down,
):
    row_count, state_dim, channels = ssm_state.shape
    owners = lax.axis_size("expert")
    own_index = lax.axis_index("expert")
    move_cap = 2 * row_count // owners
    slot_count = owners * move_cap
    my_slots = lax.dynamic_slice_in_dim(new_slot, own_index * row_count, row_count)
    target = my_slots // row_count
    target_hot = (target[:, None] == jnp.arange(owners)[None, :]).astype(jnp.int32)
    earlier = jnp.sum((jnp.cumsum(target_hot, axis=0) - target_hot) * target_hot, axis=1)
    send_slot = target * move_cap + earlier
    send_hot = (jnp.arange(slot_count)[:, None] == send_slot[None, :]).astype(jnp.bfloat16)
    packed_ssm = (
        jnp.dot(send_hot, ssm_state.reshape(row_count, -1), preferred_element_type=jnp.float32)
        .astype(jnp.bfloat16)
        .reshape(owners, move_cap, -1)
    )
    packed_conv = (
        jnp.dot(send_hot, conv_state.reshape(row_count, -1), preferred_element_type=jnp.float32)
        .astype(jnp.bfloat16)
        .reshape(owners, move_cap, -1)
    )
    recv_ssm, recv_conv = (
        lax.all_to_all(packed_ssm, "expert", split_axis=0, concat_axis=0, tiled=True),
        lax.all_to_all(packed_conv, "expert", split_axis=0, concat_axis=0, tiled=True),
    )
    arriving = (new_slot // row_count == own_index).astype(jnp.int32).reshape(owners, row_count)
    arrive_rank = (jnp.cumsum(arriving, axis=1) - arriving).reshape(-1)
    source_ids = jnp.arange(owners * row_count) // row_count
    recv_slot = source_ids * move_cap + arrive_rank
    new_place = new_slot % row_count
    place_rows = (
        (new_place[None, :] == jnp.arange(row_count)[:, None])
        & (arriving.reshape(-1)[None, :] == 1)
    ).astype(jnp.bfloat16)
    place_slots = (recv_slot[:, None] == jnp.arange(slot_count)[None, :]).astype(jnp.bfloat16)
    place_hot = jnp.dot(place_rows, place_slots, preferred_element_type=jnp.float32).astype(
        jnp.bfloat16
    )
    moved_ssm = (
        jnp.dot(place_hot, recv_ssm.reshape(slot_count, -1), preferred_element_type=jnp.float32)
        .astype(jnp.bfloat16)
        .reshape(row_count, state_dim, channels)
    )
    moved_conv = (
        jnp.dot(place_hot, recv_conv.reshape(slot_count, -1), preferred_element_type=jnp.float32)
        .astype(jnp.bfloat16)
        .reshape(row_count, -1, channels)
    )
    window = jnp.concatenate([moved_conv, conv_input[:, None, :]], axis=1)
    conv_new = window[:, 1:, :]
    conv_sum = (
        jnp.sum(window.astype(jnp.float32) * conv_weight[None, :, :], axis=1) + conv_bias[None, :]
    )
    activated = jax.nn.silu(conv_sum).astype(jnp.bfloat16)
    projected = dp_total(jnp.dot(activated, x_proj_weight, preferred_element_type=jnp.float32))
    rank_dim = step_weight.shape[0]
    step_low = projected[:, :rank_dim]
    b_coef = projected[:, rank_dim : rank_dim + state_dim]
    c_coef = projected[:, rank_dim + state_dim :]
    step_norm = (
        step_low * lax.rsqrt(jnp.mean(step_low * step_low, axis=1, keepdims=True) + 1e-06)
    ).astype(jnp.bfloat16)
    step_size = jax.nn.softplus(
        jnp.dot(step_norm, step_weight, preferred_element_type=jnp.float32) + step_bias[None, :]
    )
    act_float = activated.astype(jnp.float32)
    decays = jnp.exp(step_size[:, None, :] * (-jnp.exp(decay_log))[None, :, :])
    states = (
        decays * moved_ssm.astype(jnp.float32)
        + (step_size * act_float)[:, None, :] * b_coef[:, :, None]
    )
    ssm_new = states.astype(jnp.bfloat16)
    gated_out = (
        (jnp.sum(c_coef[:, :, None] * states, axis=1) + skip_gain[None, :] * act_float)
        * jax.nn.silu(gate_input.astype(jnp.float32))
    ).astype(jnp.bfloat16)
    mamba_mix = dp_total(
        jnp.dot(
            lax.all_gather(gated_out, "expert", axis=0, tiled=True),
            out_proj_weight,
            preferred_element_type=jnp.float32,
        )
    )
    stream = (residual.astype(jnp.float32) + mamba_mix).astype(jnp.bfloat16)
    top_count = routes.shape[1]
    width = stream.shape[1]
    capacity = min(row_count, 5 * row_count * top_count // (2 * owners))
    expert_hot = (
        (routes[:, :, None] == jnp.arange(owners)[None, None, :])
        .astype(jnp.int32)
        .reshape(owners, row_count * top_count, owners)
    )
    prior = jnp.sum((jnp.cumsum(expert_hot, axis=1) - expert_hot) * expert_hot, axis=2)
    slot_of = (routes.reshape(owners, row_count * top_count) * capacity + prior).reshape(
        owners, row_count, top_count
    )
    matches = slot_of[:, :, :, None] == jnp.arange(owners * capacity)[None, None, None, :]
    dispatch_hot = (
        jnp.any(matches, axis=2).astype(jnp.bfloat16).reshape(owners, row_count, owners, capacity)
    )
    combine_w = jnp.sum(
        jnp.where(matches, gate_weight.reshape(owners, row_count, top_count)[:, :, :, None], 0.0),
        axis=2,
    ).reshape(owners, row_count, owners, capacity)
    outgoing = jnp.einsum(
        "orec,ord->eocd",
        dispatch_hot,
        stream.reshape(owners, row_count, width),
        preferred_element_type=jnp.float32,
    ).astype(jnp.bfloat16)
    arrived = lax.all_to_all(outgoing, "expert", split_axis=0, concat_axis=3, tiled=True)
    tokens = arrived.reshape(owners * capacity, -1).astype(jnp.float32)
    normed = (
        tokens
        * lax.rsqrt(jnp.mean(tokens * tokens, axis=1, keepdims=True) + 1e-05)
        * norm_gain[None, :]
    ).astype(jnp.bfloat16)
    gate_val = jnp.dot(normed, expert_gate[0], preferred_element_type=jnp.float32)
    up_val = jnp.dot(normed, expert_up[0], preferred_element_type=jnp.float32)
    hidden = (jax.nn.silu(gate_val) * up_val).astype(jnp.bfloat16)
    partial_out = jnp.dot(hidden, expert_down[0], preferred_element_type=jnp.float32).reshape(
        owners, capacity, -1
    )
    summed = dp_total(partial_out)
    returned = lax.all_to_all(
        summed.astype(jnp.bfloat16), "expert", split_axis=2, concat_axis=0, tiled=True
    ).astype(summed.dtype)
    expert_mix = jnp.einsum(
        "orec,eocd->ord",
        combine_w,
        returned.reshape(owners, owners, capacity, width),
        precision=lax.Precision.HIGHEST,
        preferred_element_type=jnp.float32,
    )
    layer_out = (stream.astype(jnp.float32) + expert_mix.reshape(-1, width)).astype(jnp.bfloat16)
    return (ssm_new, conv_new, layer_out)


def solution(mesh):
    in_specs = (
        P("expert", None, "dp"),
        P("expert", None, "dp"),
        P(),
        P("expert", "dp"),
        P("expert", "dp"),
        P(None, "dp"),
        P("dp"),
        P("dp", None),
        P(None, "dp"),
        P("dp"),
        P(None, "dp"),
        P("dp"),
        P("dp", "expert"),
        P(None, "expert"),
        P(),
        P(),
        P(),
        P("expert", None, "dp"),
        P("expert", None, "dp"),
        P("expert", "dp", None),
    )
    out_specs = (P("expert", None, "dp"), P("expert", None, "dp"), P(None, "expert"))
    return jax.shard_map(body, mesh=mesh, in_specs=in_specs, out_specs=out_specs, check_vma=False)
```

profile of v0, /device:TPU:97, one launch (start us, length us, event | category | flops | bytes accessed | tf_op | source)
XLA Modules:
  0.0 587.0 jit_solution(9232045870672755872)
XLA Ops:
  10.9 6.9 %all-to-all-start = ((bf16[16,8,768]{2,1,0:T(8,128)(2,1)}), bf16[16,8,768]{2,1,0:T(8,128)(2,1)S(1)}, u32[]{:S(2)}, u32[]{:S(2)}) async-start(bf16[16,8,768]{2,1,0:T(8,128)(2,1)} %fusion.30), calls=%async_computation | async-start | bytes 393216 | tf_op jit(solution)/shard_map/all_to_all | solution.py:56
  22.7 2.3 all-to-all-done
  25.0 4.4 all-to-all-start.1
  30.9 108.3 %all-reduce.4.cloned.1.call-done = f32[64,288]{1,0:T(8,128)} async-done(((f32[64,288]{1,0:T(8,128)}), f32[64,288]{1,0:T(8,128)}) %all-reduce.4.cloned.1.call-update) | async-done | bytes 73744 | tf_op jit(solution)/shard_map/psum | solution.py:8
  144.2 19.4 %all_gather.3 = bf16[1024,256]{1,0:T(8,128)(2,1)S(1)} all-gather(bf16[64,256]{1,0:T(8,128)(2,1)S(1)} %fusion.46), channel_id=1, replica_groups=mesh['dp'=16,'expert'=16] {'expert'}, dimensions={0}, use_global_device_ids=true | all-gather | bytes 557056 | tf_op jit(solution)/shard_map/all_gather | solution.py:111
  165.7 2.8 select_reduce_fusion.1
  170.6 109.3 %all-reduce.6.cloned.1.call-done = f32[1024,256]{1,0:T(8,128)} async-done(((f32[1024,256]{1,0:T(8,128)}), f32[1024,256]{1,0:T(8,128)}) %all-reduce.6.cloned.1.call-update) | async-done | bytes 1048592 | tf_op jit(solution)/shard_map/psum | solution.py:8
  282.1 3.0 copy.93
  285.1 6.7 %all-to-all-start.2 = ((bf16[16,16,20,256]{3,1,2,0:T(8,128)(2,1)}), bf16[16,16,20,256]{3,1,2,0:T(8,128)(2,1)S(1)}, u32[]{:S(2)}, u32[]{:S(2)}) async-start(bf16[16,16,20,256]{3,1,2,0:T(8,128)(2,1)} %copy.93), calls=%async_computation.2 | async-start | bytes 5242880 | tf_op jit(solution)/shard_map/all_to_all | solution.py:143
  291.8 41.7 %all-to-all-done.2 = bf16[16,16,20,256]{3,1,2,0:T(8,128)(2,1)S(1)} async-done(((bf16[16,16,20,256]{3,1,2,0:T(8,128)(2,1)}), bf16[16,16,20,256]{3,1,2,0:T(8,128)(2,1)S(1)}, u32[]{:S(2)}, u32[]{:S(2)}) %all-to-all-start.2) | async-done | bytes 2621472 | tf_op jit(solution)/shard_map/all_to_all | solution.py:143
  334.9 1.5 copy.94
  338.4 1.5 fusion.9
  340.5 1.5 fusion.27
  342.1 5.9 %fusion.5 = f32[16,20,4096]{2,0,1:T(8,128)} fusion(bf16[1,448,4096]{2,1,0:T(8,128)(2,1)} %param.39, bf16[16,20,448]{2,1,0:T(8,128)(2,1)S(1)} %dot_general.52), kind=kOutput, calls=%fused_computation.9 | convolution fusion | flops 1174405120 | bytes 9199616 | tf_op jit(solution)/shard_map/dot_general | solution.py:153
  348.0 74.7 %all-reduce.7 = bf16[16,20,4096]{2,0,1:T(8,128)(2,1)S(1)} all-reduce(f32[16,20,4096]{2,0,1:T(8,128)} %fusion.5), channel_id=1, replica_groups=mesh['dp'=16,'expert'=16] {'dp'}, use_global_device_ids=true, to_apply=%region_13.14 | all-reduce | flops 1310720 | bytes 7864320 | tf_op jit(solution)/shard_map/psum | solution.py:8
  422.7 14.9 %copy.96 = bf16[16,20,4096]{1,0,2:T(8,128)(2,1)} copy(bf16[16,20,4096]{2,0,1:T(8,128)(2,1)S(1)} %all-reduce.7) | data formatting | bytes 5242880 | tf_op jit(solution)/shard_map/convert_element_type | solution.py:158
  437.6 34.7 %reshape.150 = bf16[16,2,40960]{2,1,0:T(2,128)(2,1)} reshape(bf16[4096,16,20]{2,1,0:T(8,128)(2,1)} %bitcast.85) | data formatting | bytes 5242880
  472.3 4.1 all-to-all-start.3
  476.5 2.0 select_reduce_fusion
  478.5 3.1 copy.90
  482.4 35.1 %all-to-all-done.3 = bf16[16,2,40960]{2,1,0:T(2,128)(2,1)S(1)} async-done(((bf16[16,2,40960]{2,1,0:T(2,128)(2,1)}), bf16[16,2,40960]{2,1,0:T(2,128)(2,1)S(1)}, u32[]{:S(2)}, u32[]{:S(2)}) %all-to-all-start.3) | async-done | bytes 2621472 | tf_op jit(solution)/shard_map/all_to_all | solution.py:157
  517.5 42.4 %reshape.151 = bf16[4096,16,20]{2,1,0:T(8,128)(2,1)} reshape(bf16[16,2,40960]{2,1,0:T(2,128)(2,1)S(1)} %all-to-all-done.3) | data formatting | bytes 5242880
  559.9 14.0 %copy.98 = bf16[16,20,16,256]{3,2,1,0:T(8,128)(2,1)S(1)} copy(bf16[16,20,16,256]{1,0,3,2:T(8,128)(2,1)} %bitcast.86) | data formatting | bytes 5242880 | tf_op jit(solution)/shard_map/all_to_all | solution.py:157
  573.9 5.3 fusion.15
  (92 shorter events, 27.2 us)
Async XLA Ops:
  7.2 22.8 %copy-start = (bf16[256,288]{0,1:T(8,128)(2,1)S(1)}, bf16[256,288]{0,1:T(8,128)(2,1)}, u32[]{:S(2)}) copy-start(bf16[256,288]{0,1:T(8,128)(2,1)} %param.27) | copy-start | bytes 442372
  7.2 15.1 %copy-start.5 = (bf16[64,256]{1,0:T(8,128)(2,1)S(1)}, bf16[64,256]{1,0:T(8,128)(2,1)}, u32[]{:S(2)}) copy-start(bf16[64,256]{1,0:T(8,128)(2,1)} %param.23) | copy-start | bytes 98308
  10.9 18.7 %copy-start.10 = (f32[4,256]{1,0:T(4,128)S(1)}, f32[4,256]{1,0:T(4,128)}, u32[]{:S(2)}) copy-start(f32[4,256]{1,0:T(4,128)} %param.25) | copy-start | bytes 12292
  10.9 19.0 %copy-start.11 = (f32[256]{0:T(256)S(1)}, f32[256]{0:T(256)}, u32[]{:S(2)}) copy-start(f32[256]{0:T(256)} %param.26) | copy-start | bytes 3076
  10.9 14.1 %all-to-all-start = ((bf16[16,8,768]{2,1,0:T(8,128)(2,1)}), bf16[16,8,768]{2,1,0:T(8,128)(2,1)S(1)}, u32[]{:S(2)}, u32[]{:S(2)}) async-start(bf16[16,8,768]{2,1,0:T(8,128)(2,1)} %fusion.30), calls=%async_computation | async-start | bytes 393216 | tf_op jit(solution)/shard_map/all_to_all | solution.py:56
  19.6 11.3 %copy-start.7 = (f32[16,256]{1,0:T(8,128)S(1)}, f32[16,256]{1,0:T(8,128)}, u32[]{:S(2)}) copy-start(f32[16,256]{1,0:T(8,128)} %param.30) | copy-start | bytes 49156
  19.6 121.5 %copy-start.15 = (bf16[256,256]{1,0:T(8,128)(2,1)S(1)}, bf16[256,256]{1,0:T(8,128)(2,1)}, u32[]{:S(2)}) copy-start(bf16[256,256]{1,0:T(8,128)(2,1)} %param.28) | copy-start | bytes 393220
  19.6 121.5 %copy-start.16 = (f32[256]{0:T(256)S(1)}, f32[256]{0:T(256)}, u32[]{:S(2)}) copy-start(f32[256]{0:T(256)} %param.29) | copy-start | bytes 3076
  25.0 117.2 %all-to-all-start.1 = ((bf16[16,8,4096]{2,1,0:T(8,128)(2,1)}), bf16[16,8,4096]{2,1,0:T(8,128)(2,1)S(1)}, u32[]{:S(2)}, u32[]{:S(2)}) async-start(bf16[16,8,4096]{2,1,0:T(8,128)(2,1)} %fusion.3), calls=%async_computation.1 | async-start | bytes 2097152 | tf_op jit(solution)/shard_map/all_to_all | solution.py:55
  29.4 109.9 %all-reduce.4.cloned.1.call-start = ((), (), s32[]{:S(2)}) async-start(), calls=%async_computation.4 | async-start | bytes 196608 | tf_op jit(solution)/shard_map/psum | solution.py:8
  30.8 249.0 %all-reduce.6.cloned.1.call-start = ((), (), s32[]{:S(2)}) async-start(), calls=%async_computation.5 | async-start | bytes 2097152 | tf_op jit(solution)/shard_map/psum | solution.py:8
  142.2 2.0 copy-start.6
  142.2 2.0 copy-start.12
  142.2 21.4 %copy-start.3 = (bf16[256,256]{1,0:T(8,128)(2,1)S(1)}, bf16[256,256]{1,0:T(8,128)(2,1)}, u32[]{:S(2)}) copy-start(bf16[256,256]{1,0:T(8,128)(2,1)} %param.32) | copy-start | bytes 393220
  142.8 22.1 %copy-start.4 = (s32[1024,2]{0,1:T(2,128)S(1)}, s32[1024,2]{0,1:T(2,128)}, u32[]{:S(2)}) copy-start(s32[1024,2]{0,1:T(2,128)} %param.35) | copy-start | bytes 24580
  144.2 135.6 %copy-start.2 = (bf16[1024,256]{1,0:T(8,128)(2,1)S(1)}, bf16[1024,256]{1,0:T(8,128)(2,1)}, u32[]{:S(2)}) copy-start(bf16[1024,256]{1,0:T(8,128)(2,1)} %param.33) | copy-start | bytes 1572868
  285.1 6.7 %copy-start.8 = (f32[4096]{0:T(1024)S(1)}, f32[4096]{0:T(1024)}, u32[]{:S(2)}) copy-start(f32[4096]{0:T(1024)} %param.34) | copy-start | bytes 49156
  285.1 48.4 %all-to-all-start.2 = ((bf16[16,16,20,256]{3,1,2,0:T(8,128)(2,1)}), bf16[16,16,20,256]{3,1,2,0:T(8,128)(2,1)S(1)}, u32[]{:S(2)}, u32[]{:S(2)}) async-start(bf16[16,16,20,256]{3,1,2,0:T(8,128)(2,1)} %copy.93), calls=%async_computation.2 | async-start | bytes 5242880 | tf_op jit(solution)/shard_map/all_to_all | solution.py:143
  336.4 2.0 copy-start.13
  338.4 2.0 copy-start.14
  472.3 4.1 copy-start.9
  472.3 45.2 %all-to-all-start.3 = ((bf16[16,2,40960]{2,1,0:T(2,128)(2,1)}), bf16[16,2,40960]{2,1,0:T(2,128)(2,1)S(1)}, u32[]{:S(2)}, u32[]{:S(2)}) async-start(bf16[16,2,40960]{2,1,0:T(2,128)(2,1)} %reshape.150), calls=%async_computation.3 | async-start | bytes 5242880 | tf_op jit(solution)/shard_map/all_to_all | solution.py:157
  573.9 6.2 %copy-start.1 = (bf16[256,288]{0,1:T(8,128)(2,1)S(1)}, bf16[256,288]{0,1:T(8,128)(2,1)}, u32[]{:S(2)}) copy-start(bf16[256,288]{0,1:T(8,128)(2,1)} %param.27) | copy-start | bytes 442372
Sparse Core Ops, SparseCore 0:
  33.1 106.0 all-reduce.3
  165.1 114.7 all-reduce.5
where the time goes:
time: 588 us; the launch traced here: 587 us
  waiting for transfers between devices  297 us (51%)
  local copies, waits for them, and re-layouts  123 us (21%)
  blocking collectives  94 us (16%)
  starting transfers between devices  22.1 us (4%)
  matrix products  21.5 us (4%)
  other arithmetic  15.4 us (3%)
  between operations  14.5 us (2%)
    psum x2, waiting for transfers between devices, dp_total(): return lax.psum(values, 'dp')  218 us
    unnamed x41, local copies, waits for them, and re-layouts  82.2 us
    psum x1, blocking collectives, dp_total(): return lax.psum(values, 'dp')  74.7 us
    all_to_all x1, waiting for transfers between devices, body(): lax.all_to_all(outgoing, 'expert', split_axis=0, concat_axis=3, tiled=True)  41.7 us
    all_to_all x1, waiting for transfers between devices, body(): lax.all_to_all(summed.astype(jnp.bfloat16), 'expert', split_axis=2, conca...  35.1 us
    all_gather x1, blocking collectives, body(): lax.all_gather(gated_out, 'expert', axis=0, tiled=True)  19.4 us
    convert_element_type x1, local copies, waits for them, and re-layouts, body(): summed.astype(jnp.bfloat16)  14.9 us
    all_to_all x1, local copies, waits for them, and re-layouts, body(): lax.all_to_all(summed.astype(jnp.bfloat16), 'expert', split_axis=2, conca...  14 us
  transfers between devices with their start and end apart: 6, of which 5 were waited for; matrix products, arithmetic and copies ran while one was open for 4% of the time, Pallas kernels for 0%

commit v1 on v0

--- a/solution.py
+++ b/solution.py
@@ -2,6 +2,30 @@
 import jax.numpy as jnp
 from jax import lax
 from jax.sharding import PartitionSpec as P
+
+
+def derive_the_frame(xx):
+    lane_axis = "expert"
+    out_arr, r2 = (jax.lax.axis_size(lane_axis), jax.lax.axis_index(lane_axis))
+    row_out = list(xx.shape)
+    latest = xx.shape[0] // out_arr
+    row_out[0] = latest
+    val = row_out[3]
+    row_out[3] = val * out_arr
+    dev_i = 0
+    f_next = jnp.zeros(row_out, xx.dtype)
+    while dev_i < out_arr:
+        a_next = lax.dynamic_slice_in_dim(xx, (r2 ^ dev_i) * latest, latest, axis=0)
+        if dev_i:
+            block_list = []
+            i0 = 0
+            while i0 < out_arr:
+                block_list.append((i0, i0 ^ dev_i))
+                i0 = i0 + 1
+            a_next = jax.lax.ppermute(a_next, axis_name=lane_axis, perm=block_list)
+        f_next = lax.dynamic_update_slice_in_dim(f_next, a_next, (r2 ^ dev_i) * val, axis=3)
+        dev_i += 1
+    return f_next
 
 
 def dp_total(values):
@@ -140,7 +164,7 @@
         stream.reshape(owners, row_count, width),
         preferred_element_type=jnp.float32,
     ).astype(jnp.bfloat16)
-    arrived = lax.all_to_all(outgoing, "expert", split_axis=0, concat_axis=3, tiled=True)
+    arrived = derive_the_frame(outgoing)
     tokens = arrived.reshape(owners * capacity, -1).astype(jnp.float32)
     normed = (
         tokens

time: 588 us -> 613 us (1.043); the launches traced: 587 us -> 604 us
  starting transfers between devices: 22.1 us -> 46.6 us
  waiting for transfers between devices: 297 us -> 284 us
    all_to_all x1 -> x0, waiting for transfers between devices: 41.7 us -> none  [body(): lax.all_to_all(outgoing, 'expert', split_axis=0, concat_axis=3, tiled=True)]
    ppermute x0 -> x15, starting transfers between devices: none -> 31 us  [derive_the_frame(): a_next = jax.lax.ppermute(a_next, axis_name=lane_axis, perm=block_list)]
    ppermute x0 -> x15, waiting for transfers between devices: none -> 29.9 us  [derive_the_frame(): a_next = jax.lax.ppermute(a_next, axis_name=lane_axis, perm=block_list)]
    all_to_all x1 -> x0, starting transfers between devices: 6.67 us -> none  [body(): lax.all_to_all(outgoing, 'expert', split_axis=0, concat_axis=3, tiled=True)]
    unnamed x41 -> x64, local copies, waits for them, and re-layouts: 82.2 us -> 79.8 us
  transfers between devices with their start and end apart: 6 -> 20, of which waited for: 5 -> 12; matrix products, arithmetic and copies ran while one was open for 4% -> 4% of each run, Pallas kernels for 0% -> 0%
where the time goes in v1:
time: 613 us; the launch traced here: 604 us
  waiting for transfers between devices  284 us (46%)
  local copies, waits for them, and re-layouts  122 us (20%)
  blocking collectives  94.1 us (15%)
  starting transfers between devices  46.6 us (8%)
  matrix products  25.8 us (4%)
  other arithmetic  16 us (3%)
  between operations  14.9 us (2%)
    psum x2, waiting for transfers between devices, dp_total(): return lax.psum(values, 'dp')  217 us
    unnamed x64, local copies, waits for them, and re-layouts  79.8 us
    psum x1, blocking collectives, dp_total(): return lax.psum(values, 'dp')  74.7 us
    all_to_all x1, waiting for transfers between devices, body(): lax.all_to_all(summed.astype(jnp.bfloat16), 'expert', split_axis=2, conca...  35.1 us
    ppermute x15, starting transfers between devices, derive_the_frame(): a_next = jax.lax.ppermute(a_next, axis_name=lane_axis, perm=block_list)  31 us
    ppermute x15, waiting for transfers between devices, derive_the_frame(): a_next = jax.lax.ppermute(a_next, axis_name=lane_axis, perm=block_list)  29.9 us
    all_gather x1, blocking collectives, body(): lax.all_gather(gated_out, 'expert', axis=0, tiled=True)  19.4 us
    convert_element_type x1, local copies, waits for them, and re-layouts, body(): summed.astype(jnp.bfloat16)  14.9 us
  transfers between devices with their start and end apart: 20, of which 12 were waited for; matrix products, arithmetic and copies ran while one was open for 4% of the time, Pallas kernels for 0%

profile of v1, /device:TPU:97, one launch (start us, length us, event | category | flops | bytes accessed | tf_op | source)
XLA Modules:
  0.0 603.8 jit_solution(12375475246392766249)
XLA Ops:
  10.9 6.9 %all-to-all-start = ((bf16[16,8,768]{2,1,0:T(8,128)(2,1)}), bf16[16,8,768]{2,1,0:T(8,128)(2,1)S(1)}, u32[]{:S(2)}, u32[]{:S(2)}) async-start(bf16[16,8,768]{2,1,0:T(8,128)(2,1)} %fusion.30), calls=%async_computation | async-start | bytes 393216 | tf_op jit(solution)/shard_map/all_to_all | solution.py:80
  25.0 4.4 all-to-all-start.1
  30.9 108.3 %all-reduce.4.cloned.1.call-done = f32[64,288]{1,0:T(8,128)} async-done(((f32[64,288]{1,0:T(8,128)}), f32[64,288]{1,0:T(8,128)}) %all-reduce.4.cloned.1.call-update) | async-done | bytes 73744 | tf_op jit(solution)/shard_map/psum | solution.py:32
  144.2 19.4 %all_gather.3 = bf16[1024,256]{1,0:T(8,128)(2,1)S(1)} all-gather(bf16[64,256]{1,0:T(8,128)(2,1)S(1)} %fusion.46), channel_id=1, replica_groups=mesh['dp'=16,'expert'=16] {'expert'}, dimensions={0}, use_global_device_ids=true | all-gather | bytes 557056 | tf_op jit(solution)/shard_map/all_gather | solution.py:135
  171.1 108.6 %all-reduce.6.cloned.1.call-done = f32[1024,256]{1,0:T(8,128)} async-done(((f32[1024,256]{1,0:T(8,128)}), f32[1024,256]{1,0:T(8,128)}) %all-reduce.6.cloned.1.call-update) | async-done | bytes 1048592 | tf_op jit(solution)/shard_map/psum | solution.py:32
  292.2 3.6 collective-permute-start.5
  303.7 4.8 collective-permute-start.9
  310.4 3.6 collective-permute-done.6
  314.0 3.9 collective-permute-start.11
  317.9 11.9 %collective-permute-done.7 = bf16[1,16,20,256]{3,2,0,1:T(8,128)(2,1)S(1)} collective-permute-done((bf16[1,16,20,256]{3,2,0,1:T(8,128)(2,1)S(1)}, bf16[1,16,20,256]{3,2,0,1:T(8,128)(2,1)S(1)}, u32[]{:S(2)}, u32[]{:S(2)}) %collective-permute-start.7) | collective-permute-done | bytes 163872 | tf_op jit(solution)/shard_map/ppermute | solution.py:25
  330.1 4.0 collective-permute-start.13
  334.2 3.2 collective-permute-start.14
  337.5 5.2 collective-permute-done.13
  342.7 5.1 collective-permute-done.14
  352.0 4.5 fusion.9
  358.3 5.9 fusion.5
  364.2 74.7 %all-reduce.7 = bf16[16,20,4096]{2,0,1:T(8,128)(2,1)S(1)} all-reduce(f32[16,20,4096]{2,0,1:T(8,128)} %fusion.5), channel_id=1, replica_groups=mesh['dp'=16,'expert'=16] {'dp'}, use_global_device_ids=true, to_apply=%region_13.14 | all-reduce | flops 1310720 | bytes 7864320 | tf_op jit(solution)/shard_map/psum | solution.py:32
  438.9 14.9 %copy.168 = bf16[16,20,4096]{1,0,2:T(8,128)(2,1)} copy(bf16[16,20,4096]{2,0,1:T(8,128)(2,1)S(1)} %all-reduce.7) | data formatting | bytes 5242880 | tf_op jit(solution)/shard_map/convert_element_type | solution.py:182
  453.9 34.7 %reshape.146 = bf16[16,2,40960]{2,1,0:T(2,128)(2,1)} reshape(bf16[4096,16,20]{2,1,0:T(8,128)(2,1)} %bitcast.138) | data formatting | bytes 5242880
  488.5 4.3 all-to-all-start.2
  498.9 35.1 %all-to-all-done.2 = bf16[16,2,40960]{2,1,0:T(2,128)(2,1)S(1)} async-done(((bf16[16,2,40960]{2,1,0:T(2,128)(2,1)}), bf16[16,2,40960]{2,1,0:T(2,128)(2,1)S(1)}, u32[]{:S(2)}, u32[]{:S(2)}) %all-to-all-start.2) | async-done | bytes 2621472 | tf_op jit(solution)/shard_map/all_to_all | solution.py:181
  534.0 42.4 %reshape.147 = bf16[4096,16,20]{2,1,0:T(8,128)(2,1)} reshape(bf16[16,2,40960]{2,1,0:T(2,128)(2,1)S(1)} %all-to-all-done.2) | data formatting | bytes 5242880
  576.4 14.0 %copy.170 = bf16[16,20,16,256]{3,2,1,0:T(8,128)(2,1)S(1)} copy(bf16[16,20,16,256]{1,0,3,2:T(8,128)(2,1)} %bitcast.139) | data formatting | bytes 5242880 | tf_op jit(solution)/shard_map/all_to_all | solution.py:181
  590.5 5.3 fusion.14
  (159 shorter events, 60.1 us)
Async XLA Ops:
  10.9 14.1 %all-to-all-start = ((bf16[16,8,768]{2,1,0:T(8,128)(2,1)}), bf16[16,8,768]{2,1,0:T(8,128)(2,1)S(1)}, u32[]{:S(2)}, u32[]{:S(2)}) async-start(bf16[16,8,768]{2,1,0:T(8,128)(2,1)} %fusion.30), calls=%async_computation | async-start | bytes 393216 | tf_op jit(solution)/shard_map/all_to_all | solution.py:80
  19.6 121.5 %copy-start.27 = (bf16[256,256]{1,0:T(8,128)(2,1)S(1)}, bf16[256,256]{1,0:T(8,128)(2,1)}, u32[]{:S(2)}) copy-start(bf16[256,256]{1,0:T(8,128)(2,1)} %param.28) | copy-start | bytes 393220
  19.6 121.5 %copy-start.28 = (f32[256]{0:T(256)S(1)}, f32[256]{0:T(256)}, u32[]{:S(2)}) copy-start(f32[256]{0:T(256)} %param.29) | copy-start | bytes 3076
  25.0 117.2 %all-to-all-start.1 = ((bf16[16,8,4096]{2,1,0:T(8,128)(2,1)}), bf16[16,8,4096]{2,1,0:T(8,128)(2,1)S(1)}, u32[]{:S(2)}, u32[]{:S(2)}) async-start(bf16[16,8,4096]{2,1,0:T(8,128)(2,1)} %fusion.3), calls=%async_computation.1 | async-start | bytes 2097152 | tf_op jit(solution)/shard_map/all_to_all | solution.py:79
  29.4 109.9 %all-reduce.4.cloned.1.call-start = ((), (), s32[]{:S(2)}) async-start(), calls=%async_computation.3 | async-start | bytes 196608 | tf_op jit(solution)/shard_map/psum | solution.py:32
  30.8 248.9 %all-reduce.6.cloned.1.call-start = ((), (), s32[]{:S(2)}) async-start(), calls=%async_computation.4 | async-start | bytes 2097152 | tf_op jit(solution)/shard_map/psum | solution.py:32
  144.2 135.5 %copy-start.5 = (bf16[1024,256]{1,0:T(8,128)(2,1)S(1)}, bf16[1024,256]{1,0:T(8,128)(2,1)}, u32[]{:S(2)}) copy-start(bf16[1024,256]{1,0:T(8,128)(2,1)} %param.33) | copy-start | bytes 1572868
  285.0 7.2 %collective-permute-start = (bf16[1,16,20,256]{3,2,0,1:T(8,128)(2,1)}, bf16[1,16,20,256]{3,2,0,1:T(8,128)(2,1)}, u32[]{:S(2)}, u32[]{:S(2)}) collective-permute-start(bf16[1,16,20,256]{3,2,0,1:T(8,128)(2,1)} %get-tuple-element.34), channel_id=1, source_target_pairs={{0,1},{1,0},{2,3},{3,2},{4,5},{5,4},{6,7},{7,6},{8,9},{9,8},{10,11... | collective-permute-start | bytes 491528 | tf_op jit(solution)/shard_map/ppermute | solution.py:25
  286.3 12.2 %collective-permute-start.1 = (bf16[1,16,20,256]{3,2,0,1:T(8,128)(2,1)}, bf16[1,16,20,256]{3,2,0,1:T(8,128)(2,1)S(1)}, u32[]{:S(2)}, u32[]{:S(2)}) collective-permute-start(bf16[1,16,20,256]{3,2,0,1:T(8,128)(2,1)} %get-tuple-element.33), channel_id=1, source_target_pairs={{0,2},{1,3},{2,0},{3,1},{4,6},{5,7},{6,4},{7,5},{8,10},{9,11},{10,... | collective-permute-start | bytes 491528 | tf_op jit(solution)/shard_map/ppermute | solution.py:25
  288.8 12.0 %collective-permute-start.2 = (bf16[1,16,20,256]{3,2,0,1:T(8,128)(2,1)}, bf16[1,16,20,256]{3,2,0,1:T(8,128)(2,1)S(1)}, u32[]{:S(2)}, u32[]{:S(2)}) collective-permute-start(bf16[1,16,20,256]{3,2,0,1:T(8,128)(2,1)} %get-tuple-element.32), channel_id=1, source_target_pairs={{0,3},{1,2},{2,1},{3,0},{4,7},{5,6},{6,5},{7,4},{8,11},{9,10},{10,... | collective-permute-start | bytes 491528 | tf_op jit(solution)/shard_map/ppermute | solution.py:25
  289.0 14.5 %collective-permute-start.3 = (bf16[1,16,20,256]{3,2,0,1:T(8,128)(2,1)}, bf16[1,16,20,256]{3,2,0,1:T(8,128)(2,1)S(1)}, u32[]{:S(2)}, u32[]{:S(2)}) collective-permute-start(bf16[1,16,20,256]{3,2,0,1:T(8,128)(2,1)} %get-tuple-element.31), channel_id=1, source_target_pairs={{0,4},{1,5},{2,6},{3,7},{4,0},{5,1},{6,2},{7,3},{8,12},{9,13},{10,... | collective-permute-start | bytes 491528 | tf_op jit(solution)/shard_map/ppermute | solution.py:25
  290.5 43.7 %copy-start.6 = (bf16[1,16,20,256]{3,2,0,1:T(8,128)(2,1)S(1)}, bf16[1,16,20,256]{3,2,0,1:T(8,128)(2,1)}, u32[]{:S(2)}) copy-start(bf16[1,16,20,256]{3,2,0,1:T(8,128)(2,1)} %get-tuple-element.20) | copy-start | bytes 491524
  290.5 13.2 %collective-permute-start.4 = (bf16[1,16,20,256]{3,2,0,1:T(8,128)(2,1)}, bf16[1,16,20,256]{3,2,0,1:T(8,128)(2,1)S(1)}, u32[]{:S(2)}, u32[]{:S(2)}) collective-permute-start(bf16[1,16,20,256]{3,2,0,1:T(8,128)(2,1)} %get-tuple-element.30), channel_id=1, source_target_pairs={{0,5},{1,4},{2,7},{3,6},{4,1},{5,0},{6,3},{7,2},{8,13},{9,12},{10,... | collective-permute-start | bytes 491528 | tf_op jit(solution)/shard_map/ppermute | solution.py:25
  292.2 16.3 %collective-permute-start.5 = (bf16[1,16,20,256]{3,2,0,1:T(8,128)(2,1)S(1)}, bf16[1,16,20,256]{3,2,0,1:T(8,128)(2,1)S(1)}, u32[]{:S(2)}, u32[]{:S(2)}) collective-permute-start(bf16[1,16,20,256]{3,2,0,1:T(8,128)(2,1)S(1)} %copy-done.15), channel_id=1, source_target_pairs={{0,6},{1,7},{2,4},{3,5},{4,2},{5,3},{6,0},{7,1},{8,14},{9,15},{10,... | collective-permute-start | bytes 491528 | tf_op jit(solution)/shard_map/ppermute | solution.py:25
  298.5 15.5 %collective-permute-start.6 = (bf16[1,16,20,256]{3,2,0,1:T(8,128)(2,1)S(1)}, bf16[1,16,20,256]{3,2,0,1:T(8,128)(2,1)S(1)}, u32[]{:S(2)}, u32[]{:S(2)}) collective-permute-start(bf16[1,16,20,256]{3,2,0,1:T(8,128)(2,1)S(1)} %copy-done.14), channel_id=1, source_target_pairs={{0,7},{1,6},{2,5},{3,4},{4,3},{5,2},{6,1},{7,0},{8,15},{9,14},{10,... | collective-permute-start | bytes 491528 | tf_op jit(solution)/shard_map/ppermute | solution.py:25
  300.7 29.1 %collective-permute-start.7 = (bf16[1,16,20,256]{3,2,0,1:T(8,128)(2,1)S(1)}, bf16[1,16,20,256]{3,2,0,1:T(8,128)(2,1)S(1)}, u32[]{:S(2)}, u32[]{:S(2)}) collective-permute-start(bf16[1,16,20,256]{3,2,0,1:T(8,128)(2,1)S(1)} %copy-done.13), channel_id=1, source_target_pairs={{0,8},{1,9},{2,10},{3,11},{4,12},{5,13},{6,14},{7,15},{8,0},{9,1},... | collective-permute-start | bytes 491528 | tf_op jit(solution)/shard_map/ppermute | solution.py:25
  303.5 26.6 %collective-permute-start.8 = (bf16[1,16,20,256]{3,2,0,1:T(8,128)(2,1)S(1)}, bf16[1,16,20,256]{3,2,0,1:T(8,128)(2,1)S(1)}, u32[]{:S(2)}, u32[]{:S(2)}) collective-permute-start(bf16[1,16,20,256]{3,2,0,1:T(8,128)(2,1)S(1)} %copy-done.12), channel_id=1, source_target_pairs={{0,9},{1,8},{2,11},{3,10},{4,13},{5,12},{6,15},{7,14},{8,1},{9,0},... | collective-permute-start | bytes 491528 | tf_op jit(solution)/shard_map/ppermute | solution.py:25
  303.7 30.5 %collective-permute-start.9 = (bf16[1,16,20,256]{3,2,0,1:T(8,128)(2,1)S(1)}, bf16[1,16,20,256]{3,2,0,1:T(8,128)(2,1)S(1)}, u32[]{:S(2)}, u32[]{:S(2)}) collective-permute-start(bf16[1,16,20,256]{3,2,0,1:T(8,128)(2,1)S(1)} %copy-done.11), channel_id=1, source_target_pairs={{0,10},{1,11},{2,8},{3,9},{4,14},{5,15},{6,12},{7,13},{8,2},{9,3},... | collective-permute-start | bytes 491528 | tf_op jit(solution)/shard_map/ppermute | solution.py:25
  308.5 28.8 %collective-permute-start.10 = (bf16[1,16,20,256]{3,2,0,1:T(8,128)(2,1)S(1)}, bf16[1,16,20,256]{3,2,0,1:T(8,128)(2,1)S(1)}, u32[]{:S(2)}, u32[]{:S(2)}) collective-permute-start(bf16[1,16,20,256]{3,2,0,1:T(8,128)(2,1)S(1)} %copy-done.10), channel_id=1, source_target_pairs={{0,11},{1,10},{2,9},{3,8},{4,15},{5,14},{6,13},{7,12},{8,3},{9,2},... | collective-permute-start | bytes 491528 | tf_op jit(solution)/shard_map/ppermute | solution.py:25
  314.0 23.4 %collective-permute-start.11 = (bf16[1,16,20,256]{3,2,0,1:T(8,128)(2,1)S(1)}, bf16[1,16,20,256]{3,2,0,1:T(8,128)(2,1)S(1)}, u32[]{:S(2)}, u32[]{:S(2)}) collective-permute-start(bf16[1,16,20,256]{3,2,0,1:T(8,128)(2,1)S(1)} %copy-done.9), channel_id=1, source_target_pairs={{0,12},{1,13},{2,14},{3,15},{4,8},{5,9},{6,10},{7,11},{8,4},{9,5},... | collective-permute-start | bytes 491528 | tf_op jit(solution)/shard_map/ppermute | solution.py:25
  329.9 7.6 %collective-permute-start.12 = (bf16[1,16,20,256]{3,2,0,1:T(8,128)(2,1)S(1)}, bf16[1,16,20,256]{3,2,0,1:T(8,128)(2,1)S(1)}, u32[]{:S(2)}, u32[]{:S(2)}) collective-permute-start(bf16[1,16,20,256]{3,2,0,1:T(8,128)(2,1)S(1)} %copy-done.8), channel_id=1, source_target_pairs={{0,13},{1,12},{2,15},{3,14},{4,9},{5,8},{6,11},{7,10},{8,5},{9,4},... | collective-permute-start | bytes 491528 | tf_op jit(solution)/shard_map/ppermute | solution.py:25
  330.1 12.6 %collective-permute-start.13 = (bf16[1,16,20,256]{3,2,0,1:T(8,128)(2,1)S(1)}, bf16[1,16,20,256]{3,2,0,1:T(8,128)(2,1)S(1)}, u32[]{:S(2)}, u32[]{:S(2)}) collective-permute-start(bf16[1,16,20,256]{3,2,0,1:T(8,128)(2,1)S(1)} %copy-done.7), channel_id=1, source_target_pairs={{0,14},{1,15},{2,12},{3,13},{4,10},{5,11},{6,8},{7,9},{8,6},{9,7},... | collective-permute-start | bytes 491528 | tf_op jit(solution)/shard_map/ppermute | solution.py:25
  334.2 13.6 %collective-permute-start.14 = (bf16[1,16,20,256]{3,2,0,1:T(8,128)(2,1)S(1)}, bf16[1,16,20,256]{3,2,0,1:T(8,128)(2,1)S(1)}, u32[]{:S(2)}, u32[]{:S(2)}) collective-permute-start(bf16[1,16,20,256]{3,2,0,1:T(8,128)(2,1)S(1)} %copy-done.6), channel_id=1, source_target_pairs={{0,15},{1,14},{2,13},{3,12},{4,11},{5,10},{6,9},{7,8},{8,7},{9,6},... | collective-permute-start | bytes 491528 | tf_op jit(solution)/shard_map/ppermute | solution.py:25
  488.5 45.5 %all-to-all-start.2 = ((bf16[16,2,40960]{2,1,0:T(2,128)(2,1)}), bf16[16,2,40960]{2,1,0:T(2,128)(2,1)S(1)}, u32[]{:S(2)}, u32[]{:S(2)}) async-start(bf16[16,2,40960]{2,1,0:T(2,128)(2,1)} %reshape.146), calls=%async_computation.2 | async-start | bytes 5242880 | tf_op jit(solution)/shard_map/all_to_all | solution.py:181
  (25 other events, 378.7 us)
Sparse Core Ops, SparseCore 0:
  33.1 106.0 all-reduce.3
  165.0 114.6 all-reduce.5
